TPU v7x, 32 devices: a whole 2x2x4 slice. The times are simulated.
32 devices in a mesh: user: 8 (over y, x, core), item: 4 (over z).
Axes of the slice: x: 2, y: 2, z: 4, core: 2. Of those that a mesh axis runs over, the one named last changes fastest.
Arguments:
- tokens: bfloat16 [16384, 1024], P(('user', 'item')), may hold values from -6 to 6
- lengths: int32 [32, 8], P(('user', 'item')), may hold values from 1 to 64, as said below
- destination: int32 [32, 8], P(('user', 'item')), may hold values from 0 to 7, as said below
- worker_offset: int32 [32, 8], P(('user', 'item')), may hold values from 0 to 255
- positives: int32 [16384], P(('user', 'item')), may hold values from 0 to 1023, as said below
- negatives: int32 [4, 256], replicated, may hold values from 0 to 1023, as said below
- table: bfloat16 [1024, 1024], P('item'), may hold values from -6 to 6
- in_gain: float32 [1024], replicated, may hold values from 0.1 to 1.9
- w_uvqk: bfloat16 [1024, 2048], P('item'), may hold values from -0.1875 to 0.1875
- out_gain: float32 [512], replicated, may hold values from 0.1 to 1.9
- w_out: bfloat16 [512, 1024], P(None, 'item'), may hold values from -0.25 to 0.25
Outputs:
- layer_out: bfloat16 [8192, 1024], P(('user', 'item'))
- token_grad: bfloat16 [16384, 1024], P(('user', 'item'))
- item_grad: float32 [1024, 1024], P('item', 'user')
Inputs may be any that keep to these rules, and one draw needn't show every extreme that they name: `lengths`: A device's histories lie in its rows in order from row 0 and fill at most 512 rows; every destination receives a history of exactly 64 tokens. `destination`: A device sends its 8 histories to 8 different destinations along user; the histories sent to one device by the devices of its item index, placed at their worker_offset, cover its 256 rows exactly once. `positives`: the target ids of a device lie among the 256 table rows of its item index. `negatives`: columns k * 64 to k * 64 + 63 of each group name rows held by item index k.
All inputs are finite; a program needn't handle non-finite values.
Results may differ from a plain program's by a relative error of at most 0.017.
Values may be sent and summed in bfloat16 or wider, within the bound.
A program may use at most 64 MiB of HBM per device.

v0:
```python
import jax
import jax.numpy as jnp
from jax import lax
from jax.sharding import PartitionSpec as P

HEAD = 128
TOK_DEV = 256
norm_epsilon = 1e-05
scale_epsilon = 1e-06
inverse_temp = 20.0
loss_scale = 32.0


def layer_norm(values, gain):
    center = jnp.mean(values, axis=-1, keepdims=True)
    shifted = values - center
    spread = jnp.mean(shifted * shifted, axis=-1, keepdims=True)
    return shifted * lax.rsqrt(spread + norm_epsilon) * gain


def hstu_block(rows, segment, in_gain, w_uvqk, out_gain, w_out):
    count = rows.shape[0]
    rows_f = rows.astype(jnp.float32)
    normed = layer_norm(rows_f, in_gain).astype(jnp.bfloat16)
    projected = jnp.dot(
        normed,
        lax.all_gather(w_uvqk, "item", axis=0, tiled=True),
        preferred_element_type=jnp.float32,
    )
    active = jax.nn.silu(projected).astype(jnp.bfloat16)
    width = active.shape[1] // 4
    heads = width // HEAD
    gate_u = active[:, :width]
    values_v = active[:, width : 2 * width].reshape(count, heads, HEAD)
    queries = active[:, 2 * width : 3 * width].reshape(count, heads, HEAD)
    key_rows = active[:, 3 * width :].reshape(count, heads, HEAD)
    scores = jnp.einsum(
        "qhd,khd->hqk", queries, key_rows, preferred_element_type=jnp.float32
    ) * HEAD ** (-0.5)
    order = jnp.arange(count, dtype=jnp.int32)
    allowed = (segment[:, None] == segment[None, :]) & (order[None, :] <= order[:, None])
    weights = jnp.where(allowed[None], jax.nn.silu(scores), 0.0).astype(jnp.bfloat16)
    mixed = jnp.einsum(
        "hqk,khd->qhd", weights, values_v, preferred_element_type=jnp.float32
    ).reshape(count, width)
    gated = (layer_norm(mixed, out_gain) * gate_u.astype(jnp.float32)).astype(jnp.bfloat16)
    delta = jnp.dot(
        gated, lax.all_gather(w_out, "item", axis=1, tiled=True), preferred_element_type=jnp.float32
    )
    return (rows_f + delta).astype(jnp.bfloat16)


def dispatch(rows, home_start, history_len, targets, offsets, slot_rows, user_count):
    peers = jnp.arange(user_count, dtype=jnp.int32)
    chosen = (targets[None, :] == peers[:, None]).astype(jnp.int32)
    first_row = jnp.sum(chosen * home_start[None, :], axis=1)
    sent_count = jnp.sum(chosen * history_len[None, :], axis=1)
    landing = jnp.sum(chosen * offsets[None, :], axis=1)
    within = jnp.arange(slot_rows, dtype=jnp.int32)
    picked = jnp.minimum(first_row[:, None] + within[None, :], rows.shape[0] - 1)
    filled = within[None, :] < sent_count[:, None]
    parcels = jnp.where(filled[:, :, None], rows[picked], jnp.zeros((), rows.dtype))
    labels = jnp.stack([landing, sent_count], axis=1)
    arrived, arrived_labels = (
        lax.all_to_all(parcels, "user", split_axis=0, concat_axis=0, tiled=True),
        lax.all_to_all(labels, "user", split_axis=0, concat_axis=0, tiled=True),
    )
    worker_rows = jnp.arange(TOK_DEV, dtype=jnp.int32)
    lower = arrived_labels[:, 0]
    upper = lower + arrived_labels[:, 1]
    inside = (
        (worker_rows[:, None] >= lower[None, :]) & (worker_rows[:, None] < upper[None, :])
    ).astype(jnp.int32)
    source = jnp.sum(inside * peers[None, :], axis=1)
    begin = jnp.sum(inside * lower[None, :], axis=1)
    flattened = arrived.reshape(-1, arrived.shape[-1])
    gathered = flattened[source * slot_rows + worker_rows - begin]
    return (gathered, source, arrived_labels)


def per_device(
    tokens,
    lengths,
    destination,
    worker_offset,
    positives,
    negatives,
    table,
    in_gain,
    w_uvqk,
    out_gain,
    w_out,
):
    user_count = lax.axis_size("user")
    item_count = lax.axis_size("item")
    item_here = lax.axis_index("item")
    user_here = lax.axis_index("user")
    home_rows = tokens.shape[0]
    model_width = tokens.shape[1]
    hist_count = lengths.shape[1]
    slot_rows = home_rows // hist_count
    history_len = lengths[0]
    targets = destination[0]
    offsets = worker_offset[0]
    home_start = jnp.cumsum(history_len) - history_len
    row_ids = jnp.arange(home_rows, dtype=jnp.int32)
    finished = (row_ids[:, None] >= (home_start + history_len)[None, :]).astype(jnp.int32)
    home_segment = jnp.sum(finished, axis=1)
    valid = row_ids < jnp.sum(history_len)
    home_out = hstu_block(tokens, home_segment, in_gain, w_uvqk, out_gain, w_out)
    layer_out = dispatch(
        home_out, home_start, history_len, targets, offsets, slot_rows, user_count
    )[0]
    item_rows = table.shape[0]
    table_f = table.astype(jnp.float32)
    table_scale = lax.rsqrt(jnp.mean(table_f * table_f, axis=1) + scale_epsilon)
    table_hat = table_f * table_scale[:, None]
    table_low = table_hat.astype(jnp.bfloat16)
    share = negatives.shape[1] // item_count
    owned_ids = (
        lax.dynamic_slice_in_dim(negatives, item_here * share, share, 1) - item_here * item_rows
    )
    group_rows = lax.all_to_all(
        table_low[owned_ids], "item", split_axis=0, concat_axis=0, tiled=True
    ).reshape(-1, model_width)
    positive_local = positives - item_here * item_rows
    positive_rows = table_low[positive_local]
    out_f = home_out.astype(jnp.float32)
    out_scale = lax.rsqrt(jnp.mean(out_f * out_f, axis=1) + scale_epsilon)
    out_hat = out_f * out_scale[:, None]
    out_low = out_hat.astype(jnp.bfloat16)
    factor = inverse_temp / model_width
    positive_logit = (
        jnp.einsum("rd,rd->r", out_low, positive_rows, preferred_element_type=jnp.float32) * factor
    )
    negative_logit = (
        jnp.einsum("rd,nd->rn", out_low, group_rows, preferred_element_type=jnp.float32) * factor
    )
    positive_exp = jnp.exp(positive_logit)
    negative_exp = jnp.exp(negative_logit)
    partition = positive_exp + jnp.sum(negative_exp, axis=1)
    weight = jnp.where(valid, loss_scale, 0.0)
    positive_grad = weight * (positive_exp / partition - 1.0)
    negative_grad = (weight[:, None] * negative_exp / partition[:, None]).astype(jnp.bfloat16)
    grad_hat = (
        positive_grad[:, None] * positive_rows.astype(jnp.float32)
        + jnp.dot(negative_grad, group_rows, preferred_element_type=jnp.float32)
    ) * factor
    token_grad = (
        (grad_hat - out_hat * jnp.mean(grad_hat * out_hat, axis=1, keepdims=True))
        * out_scale[:, None]
    ).astype(jnp.bfloat16)
    negative_terms = (
        jnp.einsum("rn,rd->nd", negative_grad, out_low, preferred_element_type=jnp.float32) * factor
    )
    owned_terms = lax.all_to_all(
        negative_terms.reshape(item_count, share, model_width).astype(jnp.bfloat16),
        "item",
        split_axis=0,
        concat_axis=0,
        tiled=True,
    ).astype(jnp.float32)
    positive_terms = (positive_grad * factor)[:, None] * out_low.astype(jnp.float32)
    catalog = jnp.arange(item_rows, dtype=jnp.int32)
    positive_hits = (positive_local[None, :] == catalog[:, None]).astype(jnp.float32)
    negative_hits = (owned_ids.reshape(-1)[None, :] == catalog[:, None]).astype(jnp.float32)
    row_sums = jnp.dot(positive_hits, positive_terms, precision=lax.Precision.HIGHEST)
    row_sums = row_sums + jnp.dot(
        negative_hits, owned_terms.reshape(-1, model_width), precision=lax.Precision.HIGHEST
    )
    column_width = model_width // user_count
    totals = lax.psum(row_sums.astype(jnp.bfloat16), "user").astype(jnp.float32)
    inner = jnp.mean(totals * table_hat, axis=1)
    whole = (totals - table_hat * inner[:, None]) * table_scale[:, None]
    item_grad = lax.dynamic_slice_in_dim(whole, user_here * column_width, column_width, 1)
    return (layer_out, token_grad, item_grad)


def solution(mesh):
    return jax.shard_map(
        per_device,
        mesh=mesh,
        in_specs=(
            P(("user", "item"), None),
            P(("user", "item"), None),
            P(("user", "item"), None),
            P(("user", "item"), None),
            P(("user", "item")),
            P(),
            P("item", None),
            P(),
            P("item", None),
            P(),
            P(None, "item"),
        ),
        out_specs=(P(("user", "item"), None), P(("user", "item"), None), P("item", "user")),
        check_vma=False,
    )
```

profile of v0, /device:TPU:0, one launch (start us, length us, event | category | flops | bytes accessed | tf_op | source)
XLA Modules:
  0.0 229.4 jit_solution(2644495984975450326)
XLA Ops:
  7.9 0.8 reduce-window.4
  8.8 1.4 fusion.62
  10.1 0.8 select_reduce_fusion.2
  11.7 5.2 %all-to-all-start.1 = ((s32[8,1,2]{2,1,0:T(1,128)}), s32[8,1,2]{2,1,0:T(1,128)S(1)}, u32[]{:S(2)}, u32[]{:S(2)}) async-start(s32[8,1,2]{2,1,0:T(1,128)} %copy.32), calls=%async_computation.1 | async-start | bytes 8192 | tf_op jit(solution)/shard_map/all_to_all | solution.py:66
  17.7 1.5 convert_reduce_fusion
  20.6 2.0 gather_fusion.2
  22.6 2.0 gather_fusion.3
  25.6 4.9 %all-to-all-start.2 = ((bf16[4,64,1024]{2,1,0:T(8,128)(2,1)}), bf16[4,64,1024]{2,1,0:T(8,128)(2,1)S(1)}, u32[]{:S(2)}, u32[]{:S(2)}) async-start(bf16[4,64,1024]{2,1,0:T(8,128)(2,1)} %bitcast.67), calls=%async_computation.2 | async-start | bytes 1048576 | tf_op jit(solution)/shard_map/all_to_all | solution.py:123
  30.6 73.6 %all-gather.3.cloned.1.call-done = bf16[1024,2048]{1,0:T(8,128)(2,1)} async-done(((bf16[256,2048]{1,0:T(8,128)(2,1)}), bf16[1024,2048]{1,0:T(8,128)(2,1)}) %all-gather.3.cloned.1.call-update) | async-done | bytes 4194320 | tf_op jit(solution)/shard_map/all_gather | solution.py:27
  104.2 5.1 %multiply_convert_fusion = bf16[512,2048]{1,0:T(8,128)(2,1)S(1)} fusion(bf16[1024,2048]{1,0:T(8,128)(2,1)} %all-gather.3.cloned.1.call-done, bf16[512,1024]{1,0:T(8,128)(2,1)S(1)} %copy-done.1, f32[1024]{0:T(1024)S(1)} %copy-done.8, f32[512]{0:T(512)S(1)} %add_rsqrt_fusion.2, f32[512]{0:T(512)S(1)} %broadcast_multiply_fusion.3), kind=kOutput, calls=%fused_computation.5 | convolution fusion | flops 2155347968 | bytes 7348224 | tf_op jit(solution)/shard_map/dot_general | solution.py:25
  109.3 1.3 copy-done.3
  110.6 1.2 slice_bitcast_fusion.1
  111.8 1.0 copy.38
  112.8 3.4 %fusion.63 = (f32[512]{0:T(512)S(1)}, f32[4,128,512]{2,1,0:T(8,128)S(1)}) fusion(bf16[512,4,128]{0,2,1:T(8,128)(2,1)} %bitcast.72, pred[512,512]{1,0:T(8,128)(4,1)S(1)} %fusion.34, bf16[64,4,8,128]{3,2,1,0:T(8,128)(2,1)} %get-tuple-element.15, bf16[64,4,8,128]{3,2,1,0:T(8,128)(2,1)} %get-tuple-element.14), kind=kOutput, calls=%fused_computation.121 | convolution fusion | flops 544472576 | bytes 2885632 | tf_op jit(solution)/shard_map/hqk,khd->qhd/dot_general | solution.py:43
  116.2 1.3 copy.39
  117.7 16.4 %all-gather.5.cloned.1.call-done = bf16[512,1024]{1,0:T(8,128)(2,1)} async-done(((bf16[512,256]{1,0:T(8,128)(2,1)}), bf16[512,1024]{1,0:T(8,128)(2,1)}) %all-gather.5.cloned.1.call-update) | async-done | bytes 1048592 | tf_op jit(solution)/shard_map/all_gather | solution.py:48
  134.1 3.0 %fusion.12 = (f32[512]{0:T(512)S(1)}, bf16[512,1024]{1,0:T(8,128)(2,1)S(1)}) fusion(bf16[512,1024]{1,0:T(8,128)(2,1)} %all-gather.5.cloned.1.call-done, f32[512,512]{1,0:T(8,128)} %copy.39, bf16[512,2048]{1,0:T(8,128)(2,1)} %copy-done.3, f32[512]{0:T(512)S(1)} %copy-done.9, f32[512]{0:T(512)S(1)} %add_rsqrt_fusion.1, f32[512]{0:T(512)S(1)} %broadcast_multiply_fusion.1, ...), kind=kOutput, calls=%fused_computation.26 | convolution fusion | flops 541588992 | bytes 4726784 | tf_op jit(solution)/shard_map/dot_general | solution.py:47
  138.2 0.7 broadcast_multiply_fusion
  139.0 1.3 fusion.20
  140.3 3.8 %all-to-all-start.3 = ((bf16[4,64,1024]{2,1,0:T(8,128)(2,1)}), bf16[4,64,1024]{2,1,0:T(8,128)(2,1)S(1)}, u32[]{:S(2)}, u32[]{:S(2)}) async-start(bf16[4,64,1024]{2,1,0:T(8,128)(2,1)} %bitcast.71), calls=%async_computation.3 | async-start | bytes 1048576 | tf_op jit(solution)/shard_map/all_to_all | solution.py:156
  144.2 2.8 %gather_fusion = bf16[512,1024]{1,0:T(8,128)(2,1)} fusion(bf16[512,1024]{1,0:T(8,128)(2,1)S(1)} %get-tuple-element.25, s32[1024]{0:T(1024)S(1)} %pad_clamp_fusion.3), kind=kCustom, calls=%fused_computation | custom fusion | bytes 2099200 | tf_op jit(solution)/shard_map/gather | solution.py:62
  147.0 2.4 %broadcast_select_fusion = bf16[8,64,1024]{2,1,0:T(8,128)(2,1)} fusion(bf16[8,64,1024]{2,1,0:T(8,128)(2,1)} %bitcast.65, pred[8,64]{1,0:T(8,128)(4,1)S(1)} %iota_compare_fusion.9), kind=kLoop, calls=%fused_computation.54 | loop fusion | flops 524288 | bytes 2097664 | tf_op jit(solution)/shard_map/jit(_where)/select_n | solution.py:62
  149.4 2.1 fusion.8
  151.5 5.7 %all-to-all-done.3 = bf16[4,64,1024]{2,1,0:T(8,128)(2,1)S(1)} async-done(((bf16[4,64,1024]{2,1,0:T(8,128)(2,1)}), bf16[4,64,1024]{2,1,0:T(8,128)(2,1)S(1)}, u32[]{:S(2)}, u32[]{:S(2)}) %all-to-all-start.3) | async-done | bytes 524320 | tf_op jit(solution)/shard_map/all_to_all | solution.py:156
  157.2 4.2 %all-to-all-start = ((bf16[8,64,1024]{2,1,0:T(8,128)(2,1)}), bf16[8,64,1024]{2,1,0:T(8,128)(2,1)S(1)}, u32[]{:S(2)}, u32[]{:S(2)}) async-start(bf16[8,64,1024]{2,1,0:T(8,128)(2,1)} %broadcast_select_fusion), calls=%async_computation | async-start | bytes 2097152 | tf_op jit(solution)/shard_map/all_to_all | solution.py:65
  161.8 2.4 %fusion.21 = bf16[256,1024]{1,0:T(8,128)(2,1)} fusion(f32[256,1024]{1,0:T(8,128)S(1)} %fusion.48, f32[512]{0:T(512)S(1)} %get-tuple-element.8, s32[512]{0:T(512)S(1)} %get-tuple-element.13, bf16[512,1024]{1,0:T(8,128)(2,1)S(1)} %get-tuple-element.25, f32[512]{0:T(512)S(1)} %add_rsqrt_fusion), kind=kOutput, calls=%fused_computation.38 | convolution fusion | flops 1613889536 | bytes 2627584 | tf_op jit(solution)/shard_map/dot_general | solution.py:167
  164.2 3.0 %fusion.11 = bf16[512,1024]{1,0:T(8,128)(2,1)} fusion(f32[512,1024]{1,0:T(8,128)} %get-tuple-element.29, bf16[512,1024]{1,0:T(8,128)(2,1)S(1)} %get-tuple-element.25, f32[512]{0:T(512)S(1)} %broadcast_multiply_fusion.2, f32[512]{0:T(512)S(1)} %add_rsqrt_fusion), kind=kLoop, calls=%fused_computation.25 | loop fusion | flops 3145728 | bytes 4198400 | tf_op jit(solution)/shard_map/convert_element_type | solution.py:152
  167.2 11.0 %all-to-all-done = bf16[8,64,1024]{2,1,0:T(8,128)(2,1)S(1)} async-done(((bf16[8,64,1024]{2,1,0:T(8,128)(2,1)}), bf16[8,64,1024]{2,1,0:T(8,128)(2,1)S(1)}, u32[]{:S(2)}, u32[]{:S(2)}) %all-to-all-start) | async-done | bytes 1048608 | tf_op jit(solution)/shard_map/all_to_all | solution.py:65
  178.2 2.0 gather_fusion.1
  180.2 40.3 %all-reduce.2.cloned.1.call-done = bf16[256,1024]{1,0:T(8,128)(2,1)} async-done(((bf16[256,1024]{1,0:T(8,128)(2,1)}), bf16[256,1024]{1,0:T(8,128)(2,1)}) %all-reduce.2.cloned.1.call-update) | async-done | bytes 524304 | tf_op jit(solution)/shard_map/psum | solution.py:172
  220.5 1.4 multiply_reduce_fusion
  222.0 0.8 fusion.49
  (69 shorter events, 6.5 us)
Async XLA Ops:
  7.2 12.1 %copy-start.1 = (bf16[512,1024]{1,0:T(8,128)(2,1)S(1)}, bf16[512,1024]{1,0:T(8,128)(2,1)}, u32[]{:S(2)}) copy-start(bf16[512,1024]{1,0:T(8,128)(2,1)} %param.11) | copy-start | bytes 3145732
  7.2 12.8 %copy-start.6 = (s32[512]{0:T(512)S(1)}, s32[512]{0:T(512)}, u32[]{:S(2)}) copy-start(s32[512]{0:T(512)} %param.15) | copy-start | bytes 6148
  7.2 12.8 %copy-start = (bf16[256,1024]{1,0:T(8,128)(2,1)S(1)}, bf16[256,1024]{1,0:T(8,128)(2,1)}, u32[]{:S(2)}) copy-start(bf16[256,1024]{1,0:T(8,128)(2,1)} %param.17) | copy-start | bytes 1572868
  7.2 97.0 %all-gather.3.cloned.1.call-start = ((), (), s32[]{:S(2)}) async-start(), calls=%async_computation.4 | async-start | bytes 5242880 | tf_op jit(solution)/shard_map/all_gather | solution.py:27
  11.7 13.9 %all-to-all-start.1 = ((s32[8,1,2]{2,1,0:T(1,128)}), s32[8,1,2]{2,1,0:T(1,128)S(1)}, u32[]{:S(2)}, u32[]{:S(2)}) async-start(s32[8,1,2]{2,1,0:T(1,128)} %copy.32), calls=%async_computation.1 | async-start | bytes 8192 | tf_op jit(solution)/shard_map/all_to_all | solution.py:66
  16.9 3.5 %copy-start.7 = (s32[4,256]{1,0:T(4,128)S(1)}, s32[4,256]{1,0:T(4,128)}, u32[]{:S(2)}) copy-start(s32[4,256]{1,0:T(4,128)} %param.16) | copy-start | bytes 12292
  16.9 117.2 %all-gather.5.cloned.1.call-start = ((), (), s32[]{:S(2)}) async-start(), calls=%async_computation.5 | async-start | bytes 1310720 | tf_op jit(solution)/shard_map/all_gather | solution.py:48
  22.6 81.6 %copy-start.8 = (f32[1024]{0:T(1024)S(1)}, f32[1024]{0:T(1024)}, u32[]{:S(2)}) copy-start(f32[1024]{0:T(1024)} %param.18) | copy-start | bytes 12292
  25.6 112.0 %all-to-all-start.2 = ((bf16[4,64,1024]{2,1,0:T(8,128)(2,1)}), bf16[4,64,1024]{2,1,0:T(8,128)(2,1)S(1)}, u32[]{:S(2)}, u32[]{:S(2)}) async-start(bf16[4,64,1024]{2,1,0:T(8,128)(2,1)} %bitcast.67), calls=%async_computation.2 | async-start | bytes 1048576 | tf_op jit(solution)/shard_map/all_to_all | solution.py:123
  109.3 1.4 copy-start.3
  116.2 17.9 %copy-start.9 = (f32[512]{0:T(512)S(1)}, f32[512]{0:T(512)}, u32[]{:S(2)}) copy-start(f32[512]{0:T(512)} %param.20) | copy-start | bytes 6148
  137.6 2.7 %copy-start.4 = (bf16[4,64,1024]{2,1,0:T(8,128)(2,1)}, bf16[4,64,1024]{2,1,0:T(8,128)(2,1)S(1)}, u32[]{:S(2)}) copy-start(bf16[4,64,1024]{2,1,0:T(8,128)(2,1)S(1)} %all-to-all-done.2) | copy-start | bytes 1572868
  138.2 0.8 copy-start.10
  140.3 16.9 %all-to-all-start.3 = ((bf16[4,64,1024]{2,1,0:T(8,128)(2,1)}), bf16[4,64,1024]{2,1,0:T(8,128)(2,1)S(1)}, u32[]{:S(2)}, u32[]{:S(2)}) async-start(bf16[4,64,1024]{2,1,0:T(8,128)(2,1)} %bitcast.71), calls=%async_computation.3 | async-start | bytes 1048576 | tf_op jit(solution)/shard_map/all_to_all | solution.py:156
  147.0 2.4 %copy-start.5 = (bf16[4,64,1024]{2,1,0:T(8,128)(2,1)S(1)}, bf16[4,64,1024]{2,1,0:T(8,128)(2,1)}, u32[]{:S(2)}) copy-start(bf16[4,64,1024]{2,1,0:T(8,128)(2,1)} %copy-done.4) | copy-start | bytes 1572868
  147.0 2.4 %copy-start.11 = (f32[512,256]{0,1:T(8,128)S(1)}, f32[512,256]{0,1:T(8,128)}, u32[]{:S(2)}) copy-start(f32[512,256]{0,1:T(8,128)} %copy-done.10) | copy-start | bytes 1572868
  157.2 21.0 %all-to-all-start = ((bf16[8,64,1024]{2,1,0:T(8,128)(2,1)}), bf16[8,64,1024]{2,1,0:T(8,128)(2,1)S(1)}, u32[]{:S(2)}, u32[]{:S(2)}) async-start(bf16[8,64,1024]{2,1,0:T(8,128)(2,1)} %broadcast_select_fusion), calls=%async_computation | async-start | bytes 2097152 | tf_op jit(solution)/shard_map/all_to_all | solution.py:65
  161.5 59.0 %all-reduce.2.cloned.1.call-start = ((), (), s32[]{:S(2)}) async-start(), calls=%async_computation.6 | async-start | bytes 1048576 | tf_op jit(solution)/shard_map/psum | solution.py:172
  220.5 1.4 copy-start.2
Sparse Core Ops, SparseCore 0:
  9.6 94.5 all-gather.2
  105.7 28.3 all-gather.4
  165.4 55.0 all-reduce.1
where the time goes:
time: 230 us; the launch traced here: 229 us
  waiting for transfers between devices  148 us (64%)
  starting transfers between devices  18.2 us (8%)
  matrix products  18.1 us (8%)
  other arithmetic  15.9 us (7%)
  local copies, waits for them, and re-layouts  14.7 us (6%)
  between operations  14 us (6%)
    all_gather x1, waiting for transfers between devices, hstu_block(): lax.all_gather(w_uvqk, 'item', axis=0, tiled=True)  73.6 us
    psum x1, waiting for transfers between devices, per_device(): totals = lax.psum(row_sums.astype(jnp.bfloat16), 'user').astype(jnp.float32)  40.3 us
    all_gather x1, waiting for transfers between devices, hstu_block(): lax.all_gather(w_out, 'item', axis=1, tiled=True)  16.4 us
    all_to_all x1, waiting for transfers between devices, dispatch(): lax.all_to_all(parcels, 'user', split_axis=0, concat_axis=0, tiled=True)  11 us
    all_to_all x1, waiting for transfers between devices, per_device(): lax.all_to_all(negative_terms.reshape(item_count, share, model_width).ast...  5.72 us
    all_to_all x1, starting transfers between devices, dispatch(): lax.all_to_all(labels, 'user', split_axis=0, concat_axis=0, tiled=True)  5.2 us
    dot_general x1, matrix products, hstu_block(): jnp.dot(normed, lax.all_gather(w_uvqk, 'item', axis=0, tiled=True), prefe...  5.07 us
    all_to_all x1, starting transfers between devices, per_device(): lax.all_to_all(table_low[owned_ids], 'item', split_axis=0, concat_axis=0,...  4.85 us
  transfers between devices with their start and end apart: 7, of which 5 were waited for; matrix products, arithmetic and copies ran while one was open for 18% of the time, Pallas kernels for 0%

commit v1 on v0

--- a/solution.py
+++ b/solution.py
@@ -169,7 +169,9 @@
         negative_hits, owned_terms.reshape(-1, model_width), precision=lax.Precision.HIGHEST
     )
     column_width = model_width // user_count
-    totals = lax.psum(row_sums.astype(jnp.bfloat16), "user").astype(jnp.float32)
+    totals = jnp.sum(lax.all_gather(row_sums.astype(jnp.bfloat16), "user"), axis=0).astype(
+        jnp.float32
+    )
     inner = jnp.mean(totals * table_hat, axis=1)
     whole = (totals - table_hat * inner[:, None]) * table_scale[:, None]
     item_grad = lax.dynamic_slice_in_dim(whole, user_here * column_width, column_width, 1)

time: 230 us -> 215 us (0.935)
  waiting for transfers between devices: 148 us -> 135 us
    psum x1 -> x0, waiting for transfers between devices: 40.3 us -> none  [per_device(): totals = lax.psum(row_sums.astype(jnp.bfloat16), 'user').astype(jnp.float32)]
    all_to_all x1, waiting for transfers between devices: 11 us -> 19.9 us  [dispatch(): lax.all_to_all(parcels, 'user', split_axis=0, concat_axis=0, tiled=True)]
    all_to_all x1, waiting for transfers between devices: 5.72 us -> 13 us  [per_device(): lax.all_to_all(negative_terms.reshape(item_count, share, model_width).ast...]
    all_to_all x1, waiting for transfers between devices: 0.01 us -> 4.38 us  [dispatch(): lax.all_to_all(labels, 'user', split_axis=0, concat_axis=0, tiled=True)]
    all_gather x1, waiting for transfers between devices: 73.6 us -> 77.3 us  [hstu_block(): lax.all_gather(w_uvqk, 'item', axis=0, tiled=True)]
    reduce_sum x0 -> x1, other arithmetic: none -> 3.16 us  [per_device(): jnp.sum(lax.all_gather(row_sums.astype(jnp.bfloat16), 'user'), axis=0)]
  transfers between devices with their start and end apart: 7 -> 7, of which waited for: 5 -> 6; matrix products, arithmetic and copies ran while one was open for 18% -> 16% of each run, Pallas kernels for 0% -> 0%
where the time goes in v1:
time: 215 us; the launch traced here: 214 us
  waiting for transfers between devices  135 us (63%)
  matrix products  18.9 us (9%)
  starting transfers between devices  18.2 us (8%)
  other arithmetic  14.3 us (7%)
  local copies, waits for them, and re-layouts  14 us (7%)
  between operations  14 us (7%)
    all_gather x1, waiting for transfers between devices, hstu_block(): lax.all_gather(w_uvqk, 'item', axis=0, tiled=True)  77.3 us
    all_to_all x1, waiting for transfers between devices, dispatch(): lax.all_to_all(parcels, 'user', split_axis=0, concat_axis=0, tiled=True)  19.9 us
    all_gather x1, waiting for transfers between devices, hstu_block(): lax.all_gather(w_out, 'item', axis=1, tiled=True)  17 us
    all_to_all x1, waiting for transfers between devices, per_device(): lax.all_to_all(negative_terms.reshape(item_count, share, model_width).ast...  13 us
    all_to_all x1, starting transfers between devices, per_device(): lax.all_to_all(table_low[owned_ids], 'item', split_axis=0, concat_axis=0,...  6.48 us
    dot_general x1, matrix products, hstu_block(): jnp.dot(normed, lax.all_gather(w_uvqk, 'item', axis=0, tiled=True), prefe...  5.07 us
    all_to_all x1, waiting for transfers between devices, dispatch(): lax.all_to_all(labels, 'user', split_axis=0, concat_axis=0, tiled=True)  4.38 us
  transfers between devices with their start and end apart: 7, of which 6 were waited for; matrix products, arithmetic and copies ran while one was open for 16% of the time, Pallas kernels for 0%

profile of v1, /device:TPU:0, one launch (start us, length us, event | category | flops | bytes accessed | tf_op | source)
XLA Modules:
  0.0 214.3 jit_solution(337042820895832773)
XLA Ops:
  7.9 0.8 compare_select_fusion.2
  8.8 1.2 fusion.23
  10.0 1.2 fusion.58
  11.2 2.0 gather_fusion.3
  13.2 6.5 %all-to-all-start.2 = ((bf16[4,64,1024]{2,1,0:T(8,128)(2,1)}), bf16[4,64,1024]{2,1,0:T(8,128)(2,1)}, u32[]{:S(2)}, u32[]{:S(2)}) async-start(bf16[4,64,1024]{2,1,0:T(8,128)(2,1)} %bitcast.21), calls=%async_computation.2 | async-start | bytes 1048576 | tf_op jit(solution)/shard_map/all_to_all | solution.py:123
  22.2 2.1 gather_fusion.2
  25.0 77.3 %all-gather.5.cloned.1.call-done = bf16[1024,2048]{1,0:T(8,128)(2,1)} async-done(((bf16[256,2048]{1,0:T(8,128)(2,1)}), bf16[1024,2048]{1,0:T(8,128)(2,1)}) %all-gather.5.cloned.1.call-update) | async-done | bytes 4194320 | tf_op jit(solution)/shard_map/all_gather | solution.py:27
  102.3 5.1 %multiply_convert_fusion = bf16[512,2048]{1,0:T(8,128)(2,1)S(1)} fusion(bf16[1024,2048]{1,0:T(8,128)(2,1)} %all-gather.5.cloned.1.call-done, bf16[512,1024]{1,0:T(8,128)(2,1)S(1)} %copy-done.1, f32[1024]{0:T(1024)S(1)} %copy-done.7, f32[512]{0:T(512)S(1)} %add_rsqrt_fusion.2, f32[512]{0:T(512)S(1)} %broadcast_multiply_fusion.3), kind=kOutput, calls=%fused_computation.5 | convolution fusion | flops 2155347968 | bytes 7348224 | tf_op jit(solution)/shard_map/dot_general | solution.py:25
  107.4 1.3 copy-done.2
  108.7 1.2 slice_bitcast_fusion.1
  109.9 1.0 copy.38
  110.9 3.4 %fusion.63 = (f32[512]{0:T(512)S(1)}, f32[4,128,512]{2,1,0:T(8,128)S(1)}) fusion(bf16[512,4,128]{0,2,1:T(8,128)(2,1)} %bitcast.70, pred[512,512]{1,0:T(8,128)(4,1)S(1)} %fusion.34, bf16[64,4,8,128]{3,2,1,0:T(8,128)(2,1)} %get-tuple-element.15, bf16[64,4,8,128]{3,2,1,0:T(8,128)(2,1)} %get-tuple-element.14), kind=kOutput, calls=%fused_computation.121 | convolution fusion | flops 544472576 | bytes 2885632 | tf_op jit(solution)/shard_map/hqk,khd->qhd/dot_general | solution.py:43
  114.4 1.3 copy.39
  115.9 17.0 %all-gather.7.cloned.1.call-done = bf16[512,1024]{1,0:T(8,128)(2,1)} async-done(((bf16[512,256]{1,0:T(8,128)(2,1)}), bf16[512,1024]{1,0:T(8,128)(2,1)}) %all-gather.7.cloned.1.call-update) | async-done | bytes 1048592 | tf_op jit(solution)/shard_map/all_gather | solution.py:48
  132.9 2.6 %fusion.12 = (f32[512]{0:T(512)S(1)}, bf16[512,1024]{1,0:T(8,128)(2,1)S(1)}) fusion(bf16[512,1024]{1,0:T(8,128)(2,1)} %all-gather.7.cloned.1.call-done, f32[512,512]{1,0:T(8,128)} %copy.39, bf16[512,2048]{1,0:T(8,128)(2,1)} %copy-done.2, f32[512]{0:T(512)S(1)} %copy-done.8, f32[512]{0:T(512)S(1)} %add_rsqrt_fusion.1, f32[512]{0:T(512)S(1)} %broadcast_multiply_fusion.1, ...), kind=kOutput, calls=%fused_computation.26 | convolution fusion | flops 541588992 | bytes 4726784 | tf_op jit(solution)/shard_map/dot_general | solution.py:47
  135.6 1.6 fusion.68
  138.4 1.4 fusion.20
  139.7 3.8 %all-to-all-start.3 = ((bf16[4,64,1024]{2,1,0:T(8,128)(2,1)}), bf16[4,64,1024]{2,1,0:T(8,128)(2,1)S(1)}, u32[]{:S(2)}, u32[]{:S(2)}) async-start(bf16[4,64,1024]{2,1,0:T(8,128)(2,1)} %bitcast.23), calls=%async_computation.3 | async-start | bytes 1048576 | tf_op jit(solution)/shard_map/all_to_all | solution.py:156
  143.6 13.0 %all-to-all-done.3 = bf16[4,64,1024]{2,1,0:T(8,128)(2,1)S(1)} async-done(((bf16[4,64,1024]{2,1,0:T(8,128)(2,1)}), bf16[4,64,1024]{2,1,0:T(8,128)(2,1)S(1)}, u32[]{:S(2)}, u32[]{:S(2)}) %all-to-all-start.3) | async-done | bytes 524320 | tf_op jit(solution)/shard_map/all_to_all | solution.py:156
  156.9 2.4 %fusion.21 = bf16[256,1024]{1,0:T(8,128)(2,1)} fusion(f32[256,1024]{1,0:T(8,128)S(1)} %fusion.48, f32[512]{0:T(512)S(1)} %get-tuple-element.8, s32[512]{0:T(512)S(1)} %get-tuple-element.13, bf16[512,1024]{1,0:T(8,128)(2,1)S(1)} %get-tuple-element.25, f32[512]{0:T(512)S(1)} %add_rsqrt_fusion), kind=kOutput, calls=%fused_computation.38 | convolution fusion | flops 1613889536 | bytes 2627584 | tf_op jit(solution)/shard_map/dot_general | solution.py:167
  160.2 4.3 %all-to-all-start.1 = ((s32[8,1,2]{2,1,0:T(1,128)}), s32[8,1,2]{2,1,0:T(1,128)S(1)}, u32[]{:S(2)}, u32[]{:S(2)}) async-start(s32[8,1,2]{2,1,0:T(1,128)} %copy.32), calls=%async_computation.1 | async-start | bytes 8192 | tf_op jit(solution)/shard_map/all_to_all | solution.py:66
  164.7 4.4 %all-to-all-done.1 = s32[8,1,2]{2,1,0:T(1,128)S(1)} async-done(((s32[8,1,2]{2,1,0:T(1,128)}), s32[8,1,2]{2,1,0:T(1,128)S(1)}, u32[]{:S(2)}, u32[]{:S(2)}) %all-to-all-start.1) | async-done | bytes 96 | tf_op jit(solution)/shard_map/all_to_all | solution.py:66
  169.3 2.1 gather_fusion
  171.3 1.1 broadcast_select_fusion
  172.5 3.6 %all-to-all-start = ((bf16[8,64,1024]{2,1,0:T(8,128)(2,1)}), bf16[8,64,1024]{2,1,0:T(8,128)(2,1)S(1)}, u32[]{:S(2)}, u32[]{:S(2)}) async-start(bf16[8,64,1024]{2,1,0:T(8,128)(2,1)} %broadcast_select_fusion), calls=%async_computation | async-start | bytes 2097152 | tf_op jit(solution)/shard_map/all_to_all | solution.py:65
  176.0 2.1 fusion.8
  178.1 1.4 fusion.11
  179.5 19.9 %all-to-all-done = bf16[8,64,1024]{2,1,0:T(8,128)(2,1)S(1)} async-done(((bf16[8,64,1024]{2,1,0:T(8,128)(2,1)}), bf16[8,64,1024]{2,1,0:T(8,128)(2,1)S(1)}, u32[]{:S(2)}, u32[]{:S(2)}) %all-to-all-start) | async-done | bytes 1048608 | tf_op jit(solution)/shard_map/all_to_all | solution.py:65
  199.4 2.0 gather_fusion.1
  201.4 1.9 all-gather.9.cloned.1.call-done
  203.3 3.2 %reduce_sum.174 = bf16[256,1024]{1,0:T(8,128)(2,1)S(1)} reduce(bf16[8,256,1024]{2,1,0:T(8,128)(2,1)} %bitcast.66, bf16[]{:T(256)} %constant.31.clone.1), dimensions={0}, to_apply=%region_16.17 | reduce | flops 1835008 | bytes 4718594 | tf_op jit(solution)/shard_map/reduce_sum | solution.py:172
  206.9 0.8 fusion.49
  (66 shorter events, 7.5 us)
Async XLA Ops:
  7.2 95.1 %all-gather.5.cloned.1.call-start = ((), (), s32[]{:S(2)}) async-start(), calls=%async_computation.4 | async-start | bytes 5242880 | tf_op jit(solution)/shard_map/all_gather | solution.py:27
  11.2 9.2 %copy-start.1 = (bf16[512,1024]{1,0:T(8,128)(2,1)S(1)}, bf16[512,1024]{1,0:T(8,128)(2,1)}, u32[]{:S(2)}) copy-start(bf16[512,1024]{1,0:T(8,128)(2,1)} %param.11) | copy-start | bytes 3145732
  13.2 7.9 %copy-start.4 = (s32[1,8]{1,0:T(1,128)S(1)}, s32[1,8]{1,0:T(1,128)}, u32[]{:S(2)}) copy-start(s32[1,8]{1,0:T(1,128)} %param.12) | copy-start | bytes 100
  13.2 9.0 %copy-start.3 = (s32[512]{0:T(512)S(1)}, s32[512]{0:T(512)}, u32[]{:S(2)}) copy-start(s32[512]{0:T(512)} %param.15) | copy-start | bytes 6148
  13.2 122.4 %all-to-all-start.2 = ((bf16[4,64,1024]{2,1,0:T(8,128)(2,1)}), bf16[4,64,1024]{2,1,0:T(8,128)(2,1)}, u32[]{:S(2)}, u32[]{:S(2)}) async-start(bf16[4,64,1024]{2,1,0:T(8,128)(2,1)} %bitcast.21), calls=%async_computation.2 | async-start | bytes 1048576 | tf_op jit(solution)/shard_map/all_to_all | solution.py:123
  19.7 113.2 %all-gather.7.cloned.1.call-start = ((), (), s32[]{:S(2)}) async-start(), calls=%async_computation.5 | async-start | bytes 1310720 | tf_op jit(solution)/shard_map/all_gather | solution.py:48
  22.2 80.1 %copy-start.7 = (f32[1024]{0:T(1024)S(1)}, f32[1024]{0:T(1024)}, u32[]{:S(2)}) copy-start(f32[1024]{0:T(1024)} %param.18) | copy-start | bytes 12292
  107.4 1.4 copy-start.2
  114.4 18.5 %copy-start.8 = (f32[512]{0:T(512)S(1)}, f32[512]{0:T(512)}, u32[]{:S(2)}) copy-start(f32[512]{0:T(512)} %param.20) | copy-start | bytes 6148
  137.2 2.5 %copy-start.9 = (f32[512,256]{0,1:T(8,128)}, f32[512,256]{0,1:T(8,128)S(1)}, u32[]{:S(2)}) copy-start(f32[512,256]{0,1:T(8,128)S(1)} %get-tuple-element.27) | copy-start | bytes 1572868
  139.7 16.9 %all-to-all-start.3 = ((bf16[4,64,1024]{2,1,0:T(8,128)(2,1)}), bf16[4,64,1024]{2,1,0:T(8,128)(2,1)S(1)}, u32[]{:S(2)}, u32[]{:S(2)}) async-start(bf16[4,64,1024]{2,1,0:T(8,128)(2,1)} %bitcast.23), calls=%async_computation.3 | async-start | bytes 1048576 | tf_op jit(solution)/shard_map/all_to_all | solution.py:156
  143.5 59.8 %all-gather.9.cloned.1.call-start = ((), (), s32[]{:S(2)}) async-start(), calls=%async_computation.6 | async-start | bytes 4718592 | tf_op jit(solution)/shard_map/all_gather | solution.py:172
  156.6 2.7 %copy-start.5 = (s32[1,8]{1,0:T(1,128)S(1)}, s32[1,8]{1,0:T(1,128)}, u32[]{:S(2)}) copy-start(s32[1,8]{1,0:T(1,128)} %param.14) | copy-start | bytes 100
  156.6 2.7 %copy-start.6 = (s32[1,8]{1,0:T(1,128)S(1)}, s32[1,8]{1,0:T(1,128)}, u32[]{:S(2)}) copy-start(s32[1,8]{1,0:T(1,128)} %param.13) | copy-start | bytes 100
  160.2 8.9 %all-to-all-start.1 = ((s32[8,1,2]{2,1,0:T(1,128)}), s32[8,1,2]{2,1,0:T(1,128)S(1)}, u32[]{:S(2)}, u32[]{:S(2)}) async-start(s32[8,1,2]{2,1,0:T(1,128)} %copy.32), calls=%async_computation.1 | async-start | bytes 8192 | tf_op jit(solution)/shard_map/all_to_all | solution.py:66
  172.5 26.9 %all-to-all-start = ((bf16[8,64,1024]{2,1,0:T(8,128)(2,1)}), bf16[8,64,1024]{2,1,0:T(8,128)(2,1)S(1)}, u32[]{:S(2)}, u32[]{:S(2)}) async-start(bf16[8,64,1024]{2,1,0:T(8,128)(2,1)} %broadcast_select_fusion), calls=%async_computation | async-start | bytes 2097152 | tf_op jit(solution)/shard_map/all_to_all | solution.py:65
  203.3 3.3 %copy-start = (bf16[256,1024]{1,0:T(8,128)(2,1)S(1)}, bf16[256,1024]{1,0:T(8,128)(2,1)}, u32[]{:S(2)}) copy-start(bf16[256,1024]{1,0:T(8,128)(2,1)} %param.17) | copy-start | bytes 1572868
Sparse Core Ops, SparseCore 0:
  9.5 92.7 all-gather.4
  103.9 28.9 all-gather.6
  159.4 43.8 all-gather.8
